TPU v7x, 32 devices: a whole 2x2x4 slice. The times are simulated.
32 devices in a mesh: crop: 8 (over z, x), shard: 4 (over y, core).
Axes of the slice: x: 2, y: 2, z: 4, core: 2. Of those that a mesh axis runs over, the one named last changes fastest.
Arguments:
- master: float32 [14320, 128], P('shard')
- first_moment: float32 [14320, 128], P('shard'), may hold values from -5.722046e-06 to 5.722046e-06
- second_moment: float32 [14320, 128], P('shard'), may hold values from 6.8195707e-15 to 1.0911313e-13
- step: int32 [1], replicated, may hold values from 2 to 20
- plm_table: bfloat16 [21, 1280], replicated, may hold values from -6 to 6
- plm_first: bfloat16 [1280, 5248], P('shard'), may hold values from -0.15625 to 0.15625
- plm_second: bfloat16 [2560, 1280], P('shard'), may hold values from -0.25 to 0.25
- tokens: int32 [512, 32], P(('crop', 'shard')), may hold values from 0 to 20
- lengths: int32 [512], P(('crop', 'shard')), may hold values from 12 to 32
- resolved: int32 [512, 32], P(('crop', 'shard')), may hold values 0 or 1
- coords: float32 [512, 3, 32], P(('crop', 'shard')), may hold values from -15 to 15
Outputs:
- new_master: float32 [14320, 128], P('shard')
- new_first: float32 [14320, 128], P('shard')
- new_second: float32 [14320, 128], P('shard')
- weights_low: bfloat16 [14320, 128], P('shard')
- loss: float32 [], replicated
- grad_norm: float32 [], replicated
All inputs are finite; a program needn't handle non-finite values. No bound on the sum of `resolved` on one device may be relied on, other than what follows from the above.
Results may differ from a plain program's by a relative error of at most 0.012.
The roundings to bfloat16 on the way count: a program that leaves them out, or rounds other values in their place, can miss the bound.
Values may be sent and summed in bfloat16 or wider, within the bound.
No kernel may reach another device: no remote copies, remote signals or barrier semaphores. Data moves between devices by JAX's collectives and lax.ppermute only.
A program may use at most 320 MiB of HBM per device.

v0:
```python
import jax
import jax.numpy as jnp
from jax import lax
from jax.sharding import PartitionSpec as P

NODE = 256
PAIR = 128
HEADS = 8
PAIR_HEADS = 4
PLM = 1280
PLM_FF = 2560
PLM_Z = 128
NODE_FF = 1024
PAIR_FF = 512
VOCAB = 21
BINS = 65
IPA_PTS = 4
RES = 32
MICRO = 4


beta_one = 0.9
beta_two = 0.999
learn_rate = 0.02
adam_eps = 1e-10
decay_rate = 0.01
clip_norm = 0.005
point_weight = 0.01


def layout():
    return [
        ("w_in", (PLM, NODE)),
        ("w_qkv", (NODE, 3 * NODE)),
        ("w_out", (NODE, NODE)),
        ("w_lr", (NODE, 2 * PAIR)),
        ("w_n1", (NODE, NODE_FF)),
        ("w_n2", (NODE_FF, NODE)),
        ("w_bias", (PAIR, HEADS)),
        ("w_op", (PAIR, PAIR)),
        ("w_tri", (PAIR, 5 * PAIR)),
        ("w_tri_out", (PAIR, PAIR)),
        ("w_pa", (PAIR, 4 * PAIR)),
        ("w_pa_out", (PAIR, PAIR)),
        ("w_p1", (PAIR, PAIR_FF)),
        ("w_p2", (PAIR_FF, PAIR)),
        ("w_rel", (BINS, PAIR)),
        ("w_s", (NODE, 3)),
        ("w_ipa", (NODE, 3 * NODE)),
        ("w_pts", (NODE, 6 * HEADS * IPA_PTS)),
        ("w_ipa_bias", (PAIR, HEADS)),
        ("w_ipa_out", (NODE, NODE)),
        ("w_bb", (NODE, 3)),
        ("g_node", (6, NODE)),
        ("g_pair", (6, PAIR)),
    ]


def unpack(flat):
    params = {}
    offset = 0
    for weight_name, extent in layout():
        entries = extent[0] * extent[1]
        params[weight_name] = flat[offset : offset + entries].reshape(extent)
        offset += entries
    return params


def pack(params, total):
    flat = jnp.concatenate([params[weight_name].reshape(-1) for weight_name, extent in layout()])
    return jnp.pad(flat, (0, total - flat.shape[0])).reshape(-1, 128)


def product(form, left, right):
    return jnp.einsum(
        form,
        left.astype(jnp.bfloat16),
        right.astype(jnp.bfloat16),
        preferred_element_type=jnp.float32,
    )


def passthrough(values):
    return values


def layer_norm(values, gain):
    centred = values - jnp.mean(values, axis=-1, keepdims=True)
    spread = jnp.mean(centred * centred, axis=-1, keepdims=True)
    return centred * lax.rsqrt(spread + 1e-05) * gain


def softmax_last(scores):
    expo = jnp.exp(scores - jnp.max(scores, axis=-1, keepdims=True))
    return expo / jnp.sum(expo, axis=-1, keepdims=True)


def residue_weight(lengths, resolved):
    positions = jnp.arange(resolved.shape[1])
    valid = (positions[None, :] < lengths[:, None]).astype(jnp.float32)
    first = (positions == 0).astype(jnp.float32)[None, :]
    return (jnp.maximum(resolved.astype(jnp.float32), first) * valid, valid)


def crop_loss(
    params,
    table,
    plm_first,
    plm_second,
    tokens,
    lengths,
    resolved,
    coords,
    inv_count,
    multiply,
    round_fn,
):
    crops, residues = tokens.shape
    positions = jnp.arange(residues)
    weight_res, valid = residue_weight(lengths, resolved)
    key_mask = valid[:, None, :] > 0
    pmask = (valid[:, :, None] * valid[:, None, :])[..., None]
    one_hot = (tokens[:, :, None] == jnp.arange(VOCAB)[None, None, :]).astype(jnp.float32)
    features = multiply("crv,vp->crp", one_hot, table)
    uvz = jax.nn.silu(multiply("crp,pe->cre", round_fn(layer_norm(features, 1.0)), plm_first))
    base = round_fn(uvz[..., 2 * PLM_FF :])
    plm_scores = jnp.where(
        key_mask, multiply("ciz,cjz->cij", base, base) * PLM_Z ** (-0.5), -1000000000.0
    )
    mixed = multiply(
        "cij,cje->cie", round_fn(softmax_last(plm_scores)), round_fn(uvz[..., PLM_FF : 2 * PLM_FF])
    )
    plm_out = features + multiply("cie,ep->cip", round_fn(uvz[..., :PLM_FF] * mixed), plm_second)
    node = multiply("crp,pn->crn", round_fn(layer_norm(plm_out, 1.0)), params["w_in"])
    offsets = jnp.clip(positions[None, :] - positions[:, None] + (BINS - 1) // 2, 0, BINS - 1)
    rel_hot = (offsets[:, :, None] == jnp.arange(BINS)[None, None, :]).astype(jnp.float32)
    pair = jnp.broadcast_to(
        multiply("ijb,bp->ijp", rel_hot, params["w_rel"])[None], (crops, residues, residues, PAIR)
    )
    gain_node, gain_pair = (params["g_node"], params["g_pair"])
    sides = multiply("crn,nq->crq", round_fn(layer_norm(node, gain_node[0])), params["w_lr"])
    outer = sides[:, :, None, :PAIR] * sides[:, None, :, PAIR:]
    pair = pair + multiply("cijp,pq->cijq", round_fn(outer), params["w_op"])
    tri_proj = multiply("cijp,pq->cijq", round_fn(layer_norm(pair, gain_pair[0])), params["w_tri"])
    tri_left = jax.nn.sigmoid(tri_proj[..., :PAIR]) * tri_proj[..., PAIR : 2 * PAIR] * pmask
    tri_right = (
        jax.nn.sigmoid(tri_proj[..., 2 * PAIR : 3 * PAIR])
        * tri_proj[..., 3 * PAIR : 4 * PAIR]
        * pmask
    )
    tri = multiply("cikp,cjkp->cijp", round_fn(tri_left), round_fn(tri_right))
    tri_update = multiply(
        "cijp,pq->cijq", round_fn(layer_norm(tri, gain_pair[1])), params["w_tri_out"]
    )
    pair = pair + jax.nn.sigmoid(tri_proj[..., 4 * PAIR :]) * tri_update
    pair_dim = PAIR // PAIR_HEADS
    pa_proj = multiply("cijp,pq->cijq", round_fn(layer_norm(pair, gain_pair[2])), params["w_pa"])
    pa_qkv = round_fn(pa_proj[..., : 3 * PAIR])
    pa_query = pa_qkv[..., :PAIR].reshape(crops, residues, residues, PAIR_HEADS, pair_dim)
    pa_keys = pa_qkv[..., PAIR : 2 * PAIR].reshape(crops, residues, residues, PAIR_HEADS, pair_dim)
    pa_values = pa_qkv[..., 2 * PAIR :].reshape(crops, residues, residues, PAIR_HEADS, pair_dim)
    pa_scores = multiply("cijhd,cikhd->cihjk", pa_query, pa_keys) * pair_dim ** (-0.5)
    pa_scores = jnp.where(valid[:, None, None, None, :] > 0, pa_scores, -1000000000.0)
    pa_out = multiply("cihjk,cikhd->cijhd", round_fn(softmax_last(pa_scores)), pa_values).reshape(
        crops, residues, residues, PAIR
    )
    pair = pair + multiply(
        "cijp,pq->cijq",
        round_fn(jax.nn.sigmoid(pa_proj[..., 3 * PAIR :]) * pa_out),
        params["w_pa_out"],
    )
    hidden = jax.nn.gelu(
        multiply("cijp,pf->cijf", round_fn(layer_norm(pair, gain_pair[3])), params["w_p1"]),
        approximate=True,
    )
    pair = pair + multiply("cijf,fp->cijp", round_fn(hidden), params["w_p2"])
    bias = multiply("cijp,ph->chij", round_fn(layer_norm(pair, gain_pair[4])), params["w_bias"])
    head_dim = NODE // HEADS
    qkv = round_fn(
        multiply("crn,nq->crq", round_fn(layer_norm(node, gain_node[1])), params["w_qkv"])
    )
    query = qkv[..., :NODE].reshape(crops, residues, HEADS, head_dim)
    keys = qkv[..., NODE : 2 * NODE].reshape(crops, residues, HEADS, head_dim)
    values = qkv[..., 2 * NODE :].reshape(crops, residues, HEADS, head_dim)
    scores = multiply("cihd,cjhd->chij", query, keys) * head_dim ** (-0.5) + bias
    scores = jnp.where(valid[:, None, None, :] > 0, scores, -1000000000.0)
    attended = multiply("chij,cjhd->cihd", round_fn(softmax_last(scores)), values).reshape(
        crops, residues, NODE
    )
    node = node + multiply("crn,nm->crm", round_fn(attended), params["w_out"])
    hidden_node = jax.nn.gelu(
        multiply("crn,nf->crf", round_fn(layer_norm(node, gain_node[2])), params["w_n1"]),
        approximate=True,
    )
    node = node + multiply("crf,fn->crn", round_fn(hidden_node), params["w_n2"])
    start_pos = multiply("crn,nk->crk", round_fn(layer_norm(node, gain_node[3])), params["w_s"])
    single = round_fn(layer_norm(node, gain_node[4]))
    sqkv = round_fn(multiply("crn,nq->crq", single, params["w_ipa"]))
    s_query = sqkv[..., :NODE].reshape(crops, residues, HEADS, head_dim)
    s_keys = sqkv[..., NODE : 2 * NODE].reshape(crops, residues, HEADS, head_dim)
    s_values = sqkv[..., 2 * NODE :].reshape(crops, residues, HEADS, head_dim)
    points = round_fn(multiply("crn,nq->crq", single, params["w_pts"])).reshape(
        crops, residues, 2, HEADS, IPA_PTS, 3
    )
    points = points + start_pos[:, :, None, None, None, :]
    point_diff = points[:, :, None, 0] - points[:, None, :, 1]
    dist = jnp.transpose(jnp.sum(point_diff * point_diff, axis=(-1, -2)), (0, 3, 1, 2))
    ipa_bias = multiply(
        "cijp,ph->chij", round_fn(layer_norm(pair, gain_pair[5])), params["w_ipa_bias"]
    )
    ipa_scores = (
        multiply("cihd,cjhd->chij", s_query, s_keys) * head_dim ** (-0.5)
        + ipa_bias
        - point_weight * dist
    )
    ipa_scores = jnp.where(valid[:, None, None, :] > 0, ipa_scores, -1000000000.0)
    ipa_att = multiply("chij,cjhd->cihd", round_fn(softmax_last(ipa_scores)), s_values).reshape(
        crops, residues, NODE
    )
    node = node + multiply("crn,nm->crm", round_fn(ipa_att), params["w_ipa_out"])
    predicted = start_pos + multiply(
        "crn,nk->crk", round_fn(layer_norm(node, gain_node[5])), params["w_bb"]
    )
    truth = jnp.transpose(coords, (0, 2, 1))
    pred_diff = predicted[:, :, None, :] - predicted[:, None, :, :]
    true_diff = truth[:, :, None, :] - truth[:, None, :, :]
    dist_pred = jnp.sqrt(jnp.sum(pred_diff * pred_diff, axis=-1) + 1.0)
    dist_true = jnp.sqrt(jnp.sum(true_diff * true_diff, axis=-1) + 1.0)
    error = jnp.sqrt((dist_pred - dist_true) ** 2 + 1.0) - 1.0
    pair_weight = weight_res[:, :, None] * weight_res[:, None, :]
    return jnp.sum(pair_weight * error) * inv_count


def adam_update(master, first_moment, second_moment, step, grad, norm):
    clipped = grad * jnp.minimum(1.0, clip_norm / norm)
    first = beta_one * first_moment + (1.0 - beta_one) * clipped
    second = beta_two * second_moment + (1.0 - beta_two) * clipped * clipped
    step_count = step[0].astype(jnp.float32)
    first_hat = first / (1.0 - beta_one**step_count)
    second_hat = second / (1.0 - beta_two**step_count)
    updated = master - learn_rate * (
        first_hat / (jnp.sqrt(second_hat) + adam_eps) + decay_rate * master
    )
    return (updated, first, second, updated.astype(jnp.bfloat16))


def local(
    master,
    first_moment,
    second_moment,
    step,
    plm_table,
    plm_first,
    plm_second,
    tokens,
    lengths,
    resolved,
    coords,
):
    gathered, frozen_first, frozen_second = (
        lax.all_gather(master.astype(jnp.bfloat16), "shard", axis=0, tiled=True),
        lax.all_gather(plm_first, "shard", axis=0, tiled=True),
        lax.all_gather(plm_second, "shard", axis=0, tiled=True),
    )
    params = unpack(gathered.astype(jnp.float32).reshape(-1))
    weight_res, valid = residue_weight(lengths, resolved)
    local_pairs = jnp.sum(jnp.sum(weight_res, axis=1) ** 2)
    total_pairs = lax.psum(local_pairs, ("crop", "shard"))
    inv_count = 1.0 / total_pairs
    per_micro = tokens.shape[0] // MICRO
    batches = (
        tokens.reshape(MICRO, per_micro, RES),
        lengths.reshape(MICRO, per_micro),
        resolved.reshape(MICRO, per_micro, RES),
        coords.reshape(MICRO, per_micro, 3, RES),
    )

    def micro_step(carry, batch):
        micro_tokens, micro_lengths, micro_resolved, micro_coords = batch

        def loss_of(weights):
            return crop_loss(
                weights,
                plm_table,
                frozen_first,
                frozen_second,
                micro_tokens,
                micro_lengths,
                micro_resolved,
                micro_coords,
                inv_count,
                product,
                passthrough,
            )

        value, pullback = jax.vjp(loss_of, params)
        (grads,) = pullback(jnp.float32(1.0))
        return ((jax.tree.map(jnp.add, carry[0], grads), carry[1] + value), None)

    empty_grads = jax.tree.map(jnp.zeros_like, params)
    (grads, loss_part), unused = lax.scan(micro_step, (empty_grads, jnp.float32(0.0)), batches)
    grad_rows = pack(grads, gathered.size)
    own_rows = master.shape[0]
    summed, loss = lax.psum((grad_rows, loss_part), ("crop", "shard"))
    own_grad = lax.dynamic_slice_in_dim(summed, lax.axis_index("shard") * own_rows, own_rows, 0)
    norm = jnp.sqrt(jnp.sum(summed * summed))
    updated, first, second, copy_low = adam_update(
        master, first_moment, second_moment, step, own_grad, norm
    )
    return (updated, first, second, copy_low, loss, norm)


def solution(mesh):
    placed = (
        P("shard", None),
        P("shard", None),
        P("shard", None),
        P(),
        P(),
        P("shard", None),
        P("shard", None),
        P(("crop", "shard"), None),
        P(("crop", "shard")),
        P(("crop", "shard"), None),
        P(("crop", "shard"), None, None),
    )
    return jax.shard_map(
        local,
        mesh=mesh,
        in_specs=placed,
        out_specs=(
            P("shard", None),
            P("shard", None),
            P("shard", None),
            P("shard", None),
            P(),
            P(),
        ),
        check_vma=False,
    )
```

profile of v0, /device:TPU:0, one launch (start us, length us, event | category | flops | bytes accessed | tf_op | source)
XLA Modules:
  0.0 2197.1 jit_solution(18156242039349124732)
XLA Ops:
  12.1 42.6 %psum.21 = f32[]{:T(128)} all-reduce(f32[]{:T(128)} %multiply_reduce_fusion.27), channel_id=1, replica_groups=mesh['crop'=8,'shard'=4] {'crop','shard'}, use_global_device_ids=true, to_apply=%region_2.0 | all-reduce | flops 1 | bytes 8 | tf_op jit(solution)/shard_map/psum | solution.py:268
  80.9 13.3 all-gather.7.cloned.1.call-done
  94.2 88.5 %all-gather.5.cloned.1.call-done = bf16[1280,5248]{1,0:T(8,128)(2,1)} async-done(((bf16[320,5248]{1,0:T(8,128)(2,1)}), bf16[1280,5248]{1,0:T(8,128)(2,1)}) %all-gather.5.cloned.1.call-update) | async-done | bytes 13434896 | tf_op jit(solution)/shard_map/all_gather | solution.py:262
  182.7 1803.0 %while.60 = (s32[]{:T(128)}, f32[6,256]{1,0:T(8,128)}, f32[6,128]{1,0:T(8,128)}, f32[256,3]{0,1:T(4,128)}, f32[128,8]{0,1:T(8,128)}, /*index=5*/f32[1280,256]{1,...) while((s32[]{:T(128)}, f32[6,256]{1,0:T(8,128)}, ...), condition=%wide.region_91.92_spmd.clone, body=%wide.region_3.91_spmd.clone.sunk | while | flops 12452269056 | bytes 911625600 | solution.py:301
  189.3 9.2 fusion.776
  472.9 12.2 convert_reduce_fusion.6
  485.2 9.2 convolution_convert_fusion.47
  499.0 10.0 fusion.843
  517.6 10.0 convert_bitcast_fusion.5
  922.0 12.4 convert_reduce_fusion.6
  934.4 9.2 convolution_convert_fusion.47
  948.2 9.8 fusion.843
  966.6 10.0 convert_bitcast_fusion.5
  1085.8 9.2 fusion.776
  1372.3 12.2 convert_reduce_fusion.6
  1384.5 9.2 convolution_convert_fusion.47
  1398.3 9.8 fusion.843
  1416.8 10.0 convert_bitcast_fusion.5
  1822.4 12.2 convert_reduce_fusion.6
  1834.6 9.2 convolution_convert_fusion.47
  1848.5 10.0 fusion.843
  1867.1 10.0 convert_bitcast_fusion.5
  2009.8 41.7 %psum.23 = f32[]{:T(128)} all-reduce(f32[]{:T(128)} %get-tuple-element.2691), channel_id=1, replica_groups=mesh['crop'=8,'shard'=4] {'crop','shard'}, use_global_device_ids=true, to_apply=%region_94.95 | all-reduce | flops 1 | bytes 8 | tf_op jit(solution)/shard_map/psum | solution.py:304
  2051.5 125.9 %all-reduce.35.cloned.1.call-done = f32[14320,128]{1,0:T(8,128)} async-done(((f32[14320,128]{1,0:T(8,128)}), f32[14320,128]{1,0:T(8,128)}) %all-reduce.35.cloned.1.call-update) | async-done | bytes 7331856 | tf_op jit(solution)/shard_map/psum | solution.py:304
  (3279 shorter events, 1657.5 us)
Async XLA Ops:
  7.2 48.5 %all-gather.9.cloned.1.call-start = ((), (), s32[]{:S(2)}) async-start(), calls=%async_computation.3 | async-start | bytes 4587520 | tf_op jit(solution)/shard_map/all_gather | solution.py:261
  9.8 84.4 %all-gather.7.cloned.1.call-start = ((), (), s32[]{:S(2)}) async-start(), calls=%async_computation.1 | async-start | bytes 8192000 | tf_op jit(solution)/shard_map/all_gather | solution.py:263
  10.5 172.2 %all-gather.5.cloned.1.call-start = ((), (), s32[]{:S(2)}) async-start(), calls=%async_computation | async-start | bytes 16793600 | tf_op jit(solution)/shard_map/all_gather | solution.py:262
  11.3 2166.2 %all-reduce.35.cloned.1.call-start = ((), (), s32[]{:S(2)}) async-start(), calls=%async_computation.2 | async-start | bytes 14663680 | tf_op jit(solution)/shard_map/psum | solution.py:304
  75.7 107.1 %slice-start.7 = ((bf16[14320,128]{1,0:T(8,128)(2,1)}), bf16[65,128]{1,0:T(8,128)(2,1)S(1)}, s32[]{:S(2)}) async-start(bf16[14320,128]{1,0:T(8,128)(2,1)} %reshape.1091), calls=%async_computation.11 | async-start | bytes 36864 | tf_op jit(solution)/shard_map/slice | solution.py:64
  75.7 107.1 %copy-start.181 = (bf16[21,1280]{1,0:T(8,128)(2,1)S(1)}, bf16[21,1280]{1,0:T(8,128)(2,1)}, u32[]{:S(2)}) copy-start(bf16[21,1280]{1,0:T(8,128)(2,1)} %param.17) | copy-start | bytes 161284
  183.1 120.4 %copy-start.87 = (bf16[128,512]{1,0:T(8,128)(2,1)}, bf16[128,512]{1,0:T(8,128)(2,1)S(1)}, u32[]{:S(2)}) copy-start(bf16[128,512]{1,0:T(8,128)(2,1)S(1)} %get-tuple-element.2576) | copy-start | bytes 393220 | tf_op jit(solution)/shard_map/while
  185.8 68.2 %copy-start.243 = (f32[128]{0:T(128)}, f32[128]{0:T(128)S(1)}, u32[]{:S(2)}) copy-start(f32[128]{0:T(128)S(1)} %get-tuple-element.2274) | copy-start | bytes 1540 | tf_op jit(solution)/shard_map/while
  185.8 75.1 %copy-start.227 = (f32[128]{0:T(128)}, f32[128]{0:T(128)S(1)}, u32[]{:S(2)}) copy-start(f32[128]{0:T(128)S(1)} %get-tuple-element.2279) | copy-start | bytes 1540 | tf_op jit(solution)/shard_map/while
  185.8 117.7 %copy-start.199 = (f32[128]{0:T(128)}, f32[128]{0:T(128)S(1)}, u32[]{:S(2)}) copy-start(f32[128]{0:T(128)S(1)} %get-tuple-element.2289) | copy-start | bytes 1540 | tf_op jit(solution)/shard_map/while
  206.1 226.7 %copy-start.24 = (f32[4,32,256]{2,1,0:T(8,128)}, f32[4,32,256]{2,1,0:T(8,128)S(1)}, u32[]{:S(2)}) copy-start(f32[4,32,256]{2,1,0:T(8,128)S(1)} %get-tuple-element.2261) | copy-start | bytes 393220 | tf_op jit(solution)/shard_map/while
  629.6 120.1 %copy-start.87 = (bf16[128,512]{1,0:T(8,128)(2,1)}, bf16[128,512]{1,0:T(8,128)(2,1)S(1)}, u32[]{:S(2)}) copy-start(bf16[128,512]{1,0:T(8,128)(2,1)S(1)} %get-tuple-element.2576) | copy-start | bytes 393220 | tf_op jit(solution)/shard_map/while
  632.3 74.7 %copy-start.227 = (f32[128]{0:T(128)}, f32[128]{0:T(128)S(1)}, u32[]{:S(2)}) copy-start(f32[128]{0:T(128)S(1)} %get-tuple-element.2279) | copy-start | bytes 1540 | tf_op jit(solution)/shard_map/while
  632.3 117.4 %copy-start.199 = (f32[128]{0:T(128)}, f32[128]{0:T(128)S(1)}, u32[]{:S(2)}) copy-start(f32[128]{0:T(128)S(1)} %get-tuple-element.2289) | copy-start | bytes 1540 | tf_op jit(solution)/shard_map/while
  652.5 227.2 %copy-start.24 = (f32[4,32,256]{2,1,0:T(8,128)}, f32[4,32,256]{2,1,0:T(8,128)S(1)}, u32[]{:S(2)}) copy-start(f32[4,32,256]{2,1,0:T(8,128)S(1)} %get-tuple-element.2261) | copy-start | bytes 393220 | tf_op jit(solution)/shard_map/while
  1079.6 120.5 %copy-start.87 = (bf16[128,512]{1,0:T(8,128)(2,1)}, bf16[128,512]{1,0:T(8,128)(2,1)S(1)}, u32[]{:S(2)}) copy-start(bf16[128,512]{1,0:T(8,128)(2,1)S(1)} %get-tuple-element.2576) | copy-start | bytes 393220 | tf_op jit(solution)/shard_map/while
  1082.3 74.8 %copy-start.227 = (f32[128]{0:T(128)}, f32[128]{0:T(128)S(1)}, u32[]{:S(2)}) copy-start(f32[128]{0:T(128)S(1)} %get-tuple-element.2279) | copy-start | bytes 1540 | tf_op jit(solution)/shard_map/while
  1082.3 117.8 %copy-start.199 = (f32[128]{0:T(128)}, f32[128]{0:T(128)S(1)}, u32[]{:S(2)}) copy-start(f32[128]{0:T(128)S(1)} %get-tuple-element.2289) | copy-start | bytes 1540 | tf_op jit(solution)/shard_map/while
  1102.5 227.4 %copy-start.24 = (f32[4,32,256]{2,1,0:T(8,128)}, f32[4,32,256]{2,1,0:T(8,128)S(1)}, u32[]{:S(2)}) copy-start(f32[4,32,256]{2,1,0:T(8,128)S(1)} %get-tuple-element.2261) | copy-start | bytes 393220 | tf_op jit(solution)/shard_map/while
  1529.7 120.4 %copy-start.87 = (bf16[128,512]{1,0:T(8,128)(2,1)}, bf16[128,512]{1,0:T(8,128)(2,1)S(1)}, u32[]{:S(2)}) copy-start(bf16[128,512]{1,0:T(8,128)(2,1)S(1)} %get-tuple-element.2576) | copy-start | bytes 393220 | tf_op jit(solution)/shard_map/while
  1532.4 75.0 %copy-start.227 = (f32[128]{0:T(128)}, f32[128]{0:T(128)S(1)}, u32[]{:S(2)}) copy-start(f32[128]{0:T(128)S(1)} %get-tuple-element.2279) | copy-start | bytes 1540 | tf_op jit(solution)/shard_map/while
  1532.4 117.7 %copy-start.199 = (f32[128]{0:T(128)}, f32[128]{0:T(128)S(1)}, u32[]{:S(2)}) copy-start(f32[128]{0:T(128)S(1)} %get-tuple-element.2289) | copy-start | bytes 1540 | tf_op jit(solution)/shard_map/while
  1552.7 227.5 %copy-start.24 = (f32[4,32,256]{2,1,0:T(8,128)}, f32[4,32,256]{2,1,0:T(8,128)S(1)}, u32[]{:S(2)}) copy-start(f32[4,32,256]{2,1,0:T(8,128)S(1)} %get-tuple-element.2261) | copy-start | bytes 393220 | tf_op jit(solution)/shard_map/while
  2051.5 131.4 %copy-start.127 = (f32[3580,128]{1,0:T(8,128)S(1)}, f32[3580,128]{1,0:T(8,128)}, u32[]{:S(2)}) copy-start(f32[3580,128]{1,0:T(8,128)} %param.13) | copy-start | bytes 5498884
  (1050 other events, 4667.9 us)
Sparse Core Ops, SparseCore 0:
  10.1 34.4 all-gather.8
  46.2 47.9 all-gather.6
  95.8 86.9 all-gather.4
  2009.2 168.2 all-reduce.34
where the time goes:
time: 2210 us; the launch traced here: 2200 us
  matrix products  784 us (35%)
  local copies, waits for them, and re-layouts  618 us (28%)
  other arithmetic  437 us (20%)
  waiting for transfers between devices  229 us (10%)
  blocking collectives  84.3 us (4%)
  loops' own time  25.8 us (1%)
    dot_general x344, matrix products, product(): jnp.einsum(form, left.astype(jnp.bfloat16), right.astype(jnp.bfloat16), p...  780 us
    psum x1, waiting for transfers between devices, local(): summed, loss = lax.psum((grad_rows, loss_part), ('crop', 'shard'))  126 us
    convert_element_type x56, local copies, waits for them, and re-layouts, product(): right.astype(jnp.bfloat16)  125 us
    convert_element_type x28, local copies, waits for them, and re-layouts, product(): left.astype(jnp.bfloat16)  89.2 us
    all_gather x1, waiting for transfers between devices, local(): lax.all_gather(plm_first, 'shard', axis=0, tiled=True)  88.5 us
    dot_general x28, local copies, waits for them, and re-layouts, product(): jnp.einsum(form, left.astype(jnp.bfloat16), right.astype(jnp.bfloat16), p...  84.9 us
    reduce_sum x28, other arithmetic, layer_norm(): return centred * lax.rsqrt(spread + 1e-05) * gain  80.5 us
    while x2096, local copies, waits for them, and re-layouts  50 us
  transfers between devices with their start and end apart: 4, of which 3 were waited for; matrix products, arithmetic and copies ran while one was open for 1% of the time, Pallas kernels for 0%

commit v1 on v0

v1 whole, which is shorter than its diff:
```python
import jax
import jax.numpy as jnp
from jax import lax
from jax.experimental import pallas as pl
from jax.experimental.pallas import tpu as pltpu
from jax.sharding import PartitionSpec as P

NODE = 256
PAIR = 128
HEADS = 8
PAIR_HEADS = 4
PLM = 1280
PLM_FF = 2560
PLM_Z = 128
NODE_FF = 1024
PAIR_FF = 512
VOCAB = 21
BINS = 65
IPA_PTS = 4
RES = 32
MICRO = 4


beta_one = 0.9
beta_two = 0.999
learn_rate = 0.02
adam_eps = 1e-10
decay_rate = 0.01
clip_norm = 0.005
point_weight = 0.01


BF = jnp.bfloat16
F32 = jnp.float32


def layout():
    return [
        ("w_in", (PLM, NODE)),
        ("w_qkv", (NODE, 3 * NODE)),
        ("w_out", (NODE, NODE)),
        ("w_lr", (NODE, 2 * PAIR)),
        ("w_n1", (NODE, NODE_FF)),
        ("w_n2", (NODE_FF, NODE)),
        ("w_bias", (PAIR, HEADS)),
        ("w_op", (PAIR, PAIR)),
        ("w_tri", (PAIR, 5 * PAIR)),
        ("w_tri_out", (PAIR, PAIR)),
        ("w_pa", (PAIR, 4 * PAIR)),
        ("w_pa_out", (PAIR, PAIR)),
        ("w_p1", (PAIR, PAIR_FF)),
        ("w_p2", (PAIR_FF, PAIR)),
        ("w_rel", (BINS, PAIR)),
        ("w_s", (NODE, 3)),
        ("w_ipa", (NODE, 3 * NODE)),
        ("w_pts", (NODE, 6 * HEADS * IPA_PTS)),
        ("w_ipa_bias", (PAIR, HEADS)),
        ("w_ipa_out", (NODE, NODE)),
        ("w_bb", (NODE, 3)),
        ("g_node", (6, NODE)),
        ("g_pair", (6, PAIR)),
    ]


def unpack(flat):
    params = {}
    offset = 0
    for weight_name, extent in layout():
        entries = extent[0] * extent[1]
        params[weight_name] = flat[offset : offset + entries].reshape(extent)
        offset += entries
    return params


def pack(params, total):
    flat = jnp.concatenate([params[weight_name].reshape(-1) for weight_name, extent in layout()])
    return jnp.pad(flat, (0, total - flat.shape[0])).reshape(-1, 128)


def product(form, left, right):
    return jnp.einsum(
        form,
        left.astype(jnp.bfloat16),
        right.astype(jnp.bfloat16),
        preferred_element_type=jnp.float32,
    )


def layer_norm(values, gain):
    centred = values - jnp.mean(values, axis=-1, keepdims=True)
    spread = jnp.mean(centred * centred, axis=-1, keepdims=True)
    return centred * lax.rsqrt(spread + 1e-05) * gain


def softmax_last(scores):
    expo = jnp.exp(scores - jnp.max(scores, axis=-1, keepdims=True))
    return expo / jnp.sum(expo, axis=-1, keepdims=True)


def residue_weight(lengths, resolved):
    positions = jnp.arange(resolved.shape[1])
    valid = (positions[None, :] < lengths[:, None]).astype(jnp.float32)
    first = (positions == 0).astype(jnp.float32)[None, :]
    return (jnp.maximum(resolved.astype(jnp.float32), first) * valid, valid)


PH = 4
RB = 8
M = RB * RES
EPS = 1e-05
NEG = -1000000000.0


def nn(a, b):
    return lax.dot_general(a, b, (((1,), (0,)), ((), ())), preferred_element_type=F32)


def nt(a, b):
    return lax.dot_general(a, b, (((1,), (1,)), ((), ())), preferred_element_type=F32)


def tn(a, b):
    return lax.dot_general(a, b, (((0,), (0,)), ((), ())), preferred_element_type=F32)


def ln_stats(x):
    mean = jnp.sum(x, axis=-1, keepdims=True) * (1.0 / x.shape[-1])
    c = x - mean
    var = jnp.sum(c * c, axis=-1, keepdims=True) * (1.0 / x.shape[-1])
    r = lax.rsqrt(var + EPS)
    return c * r, r


def ln_back(dxh, xh, r):
    n = 1.0 / dxh.shape[-1]
    m1 = jnp.sum(dxh, axis=-1, keepdims=True) * n
    m2 = jnp.sum(dxh * xh, axis=-1, keepdims=True) * n
    return r * (dxh - m1 - xh * m2)


def sigmoid(x):
    return 0.5 * jnp.tanh(0.5 * x) + 0.5


def gelu_parts(x):
    c = 0.7978845608028654
    x2 = x * x
    t = jnp.tanh(x * (c + (c * 0.044715) * x2))
    h = 0.5 * x * (1.0 + t)
    d = 0.5 * (1.0 + t) + 0.5 * x * (1.0 - t * t) * (c + (3.0 * c * 0.044715) * x2)
    return h, d


def head_mask(rows, dim=32):
    r = lax.broadcasted_iota(jnp.int32, (rows, PAIR), 0) // (rows // PH)
    l = lax.broadcasted_iota(jnp.int32, (rows, PAIR), 1) // dim
    return r == l


def block_diag(k, mask):
    t = jnp.concatenate([k, k, k, k], axis=0)
    return jnp.where(mask, t, jnp.zeros_like(t))


def seg_max(s, lane_head):
    out = None
    for h in range(PH):
        m = jnp.max(jnp.where(lane_head == h, s, -jnp.inf), axis=-1, keepdims=True)
        out = jnp.broadcast_to(m, s.shape) if out is None else jnp.where(lane_head == h, m, out)
    return out


def fwd_kernel(len_ref, sides_ref, rel_ref, w_op, w_tri, w_to, w_pa, w_po, w_p1, w_p2, w_bb, g_ref,
               bias_ref, p0_ref, p1_ref, p2_ref, p3_ref, tri_ref, gt_ref, pa_ref, hh_ref,
               b_scr, a_scr):
    c = pl.program_id(0)
    length = len_ref[c]
    nchunk = (length + RB - 1) // RB
    g = [g_ref[i:i + 1, :] for i in range(6)]
    jpos = lax.broadcasted_iota(jnp.int32, (RES, PAIR), 0)
    jmask = (jpos < length).astype(F32)
    lane = lax.broadcasted_iota(jnp.int32, (RES, PAIR), 1)
    lane_head = lane // 32
    key_ok = (lane % 32) < length
    hmask = head_mask(PAIR)
    ones_bd = hmask.astype(BF)

    @pl.when(nchunk < RES // RB)
    def _():
        b_scr[...] = jnp.zeros_like(b_scr)
        p0_ref[...] = jnp.zeros_like(p0_ref)
        p1_ref[...] = jnp.zeros_like(p1_ref)
        p2_ref[...] = jnp.zeros_like(p2_ref)
        p3_ref[...] = jnp.zeros_like(p3_ref)
        tri_ref[...] = jnp.zeros_like(tri_ref)
        gt_ref[...] = jnp.zeros_like(gt_ref)
        pa_ref[...] = jnp.zeros_like(pa_ref)
        hh_ref[...] = jnp.zeros_like(hh_ref)
        bias_ref[...] = jnp.zeros_like(bias_ref)

    right = sides_ref[0, :, PAIR:]

    def phase1(ci, _):
        i0 = pl.multiple_of(ci * RB, RB)
        r0 = pl.multiple_of(ci * M, M)
        rows = pl.ds(r0, M)
        left = sides_ref[0, pl.ds(i0, RB), :PAIR]
        outer = (left[:, None, :] * right[None]).reshape(M, PAIR).astype(BF)
        rel = jnp.concatenate([rel_ref[pl.ds(32 - (i0 + k), RES), :] for k in range(RB)], axis=0)
        p0 = nn(outer, w_op[...]) + rel
        p0_ref[0, rows, :] = p0
        xh, _ = ln_stats(p0)
        t = nn((xh * g[0]).astype(BF), w_tri[...])
        ipos = i0 + lax.broadcasted_iota(jnp.int32, (RB, RES, PAIR), 0)
        pm = (jmask[None] * (ipos < length).astype(F32)).reshape(M, PAIR)
        sa = sigmoid(t[:, :PAIR])
        a = (sa * t[:, PAIR:2 * PAIR] * pm).astype(BF)
        sb = sigmoid(t[:, 2 * PAIR:3 * PAIR])
        b = (sb * t[:, 3 * PAIR:4 * PAIR] * pm).astype(BF)
        st = sigmoid(t[:, 4 * PAIR:])
        gt_ref[0, rows, 0:128] = sa.astype(BF)
        gt_ref[0, rows, 128:256] = a
        gt_ref[0, rows, 256:384] = sb.astype(BF)
        gt_ref[0, rows, 384:512] = b
        gt_ref[0, rows, 512:640] = st.astype(BF)
        a_scr[rows, :] = a.astype(F32)
        b_scr[rows, :] = b.astype(F32)
        return 0

    lax.fori_loop(0, nchunk, phase1, 0)

    IB = 4

    def tri_rows(ib, _):
        i0 = ib * IB
        acc = [jnp.zeros((RES, PAIR), F32) for _ in range(IB)]
        for k in range(RES):
            bt = b_scr[pl.ds(k, RES, stride=RES), :]
            for u in range(IB):
                acc[u] = acc[u] + a_scr[pl.ds((i0 + u) * RES + k, 1), :] * bt
        for u in range(IB):
            tri_ref[0, pl.ds(pl.multiple_of((i0 + u) * RES, RES), RES), :] = acc[u]
        return 0

    lax.fori_loop(0, nchunk * (RB // IB), tri_rows, 0)

    def phase2(ci, _):
        r0 = pl.multiple_of(ci * M, M)
        rows = pl.ds(r0, M)
        xt, _ = ln_stats(tri_ref[0, rows, :])
        u = nn((xt * g[1]).astype(BF), w_to[...])
        p1 = p0_ref[0, rows, :] + gt_ref[0, rows, 512:640].astype(F32) * u
        p1_ref[0, rows, :] = p1
        x2, _ = ln_stats(p1)
        pa = nn((x2 * g[2]).astype(BF), w_pa[...])
        qkv = pa[:, :384].astype(BF)
        sg = sigmoid(pa[:, 384:])
        pa_ref[0, rows, 0:384] = qkv
        pa_ref[0, rows, 384:512] = sg.astype(BF)
        outs = []
        for i in range(RB):
            sl = slice(i * RES, (i + 1) * RES)
            kbd = block_diag(qkv[sl, 128:256], hmask)
            s = nt(qkv[sl, :128], kbd) * (32.0 ** -0.5)
            s = jnp.where(key_ok, s, NEG)
            e = jnp.exp(s - seg_max(s, lane_head)).astype(BF)
            rhs = jnp.concatenate([block_diag(qkv[sl, 256:384], hmask), ones_bd], axis=1)
            o2 = nn(e, rhs)
            inv = 1.0 / o2[:, PAIR:]
            o = o2[:, :PAIR] * inv
            outs.append(o)
            pa_ref[0, pl.ds(pl.multiple_of(r0 + i * RES, RES), RES), 512:640] = (e.astype(F32) * inv).astype(BF)
        o = jnp.concatenate(outs, axis=0)
        pa_ref[0, rows, 640:768] = o.astype(BF)
        p2 = p1 + nn((sg * o).astype(BF), w_po[...])
        p2_ref[0, rows, :] = p2
        x3, _ = ln_stats(p2)
        hpre = nn((x3 * g[3]).astype(BF), w_p1[...])
        h, hd = gelu_parts(hpre)
        hb = h.astype(BF)
        hh_ref[0, rows, 0:512] = hb
        hh_ref[0, rows, 512:1024] = hd.astype(BF)
        p3 = p2 + nn(hb, w_p2[...])
        p3_ref[0, rows, :] = p3
        x4, _ = ln_stats(p3)
        xx = jnp.concatenate([(x4 * g[4]).astype(BF), (x4 * g[5]).astype(BF)], axis=1)
        bias_ref[0, :, rows] = nt(w_bb[...], xx)
        return 0

    lax.fori_loop(0, nchunk, phase2, 0)


def full(shape):
    n = len(shape)
    return pl.BlockSpec(shape, lambda c, *_: (0,) * n)


def per_crop(shape):
    n = len(shape)
    return pl.BlockSpec((1,) + shape, lambda c, *_: (c,) + (0,) * n)


def pair_forward(lengths, sides, rel, w_op, w_tri, w_to, w_pa, w_po, w_p1, w_p2, w_bb, gains):
    crops = sides.shape[0]
    n = RES * RES
    outs = [((16, n), F32), ((n, 128), F32), ((n, 128), F32), ((n, 128), F32), ((n, 128), F32), ((n, 128), F32),
            ((n, 640), BF), ((n, 768), BF), ((n, 1024), BF)]
    ws = [rel, w_op, w_tri, w_to, w_pa, w_po, w_p1, w_p2, w_bb, gains]
    return pl.pallas_call(
        fwd_kernel,
        grid_spec=pltpu.PrefetchScalarGridSpec(
            num_scalar_prefetch=1,
            grid=(crops,),
            in_specs=[per_crop((RES, 256))] + [full(w.shape) for w in ws],
            out_specs=[per_crop(s) for s, _ in outs],
            scratch_shapes=[pltpu.VMEM((n, 128), F32), pltpu.VMEM((n, 128), F32)],
        ),
        out_shape=[jax.ShapeDtypeStruct((crops,) + s, d) for s, d in outs],
        compiler_params=pltpu.CompilerParams(vmem_limit_bytes=58 << 20),
        name="pair_fwd",
    )(lengths, sides, *ws)


def bwd_kernel(len_ref, dbt_ref, db_ref, sides_ref, p0_ref, p1_ref, p2_ref, p3_ref, tri_ref, gt_ref, pa_ref, hh_ref,
               w_op, w_tri, w_to, w_pa, w_po, w_p1, w_p2, w_bb, g_ref,
               dsides_ref, d_op, d_tri, d_to, d_pa, d_po, d_p1, d_p2t, d_bb, d_g, d_rel,
               a_scr, b_scr, dt_scr, dp_scr, dtg_scr):
    c = pl.program_id(0)
    length = len_ref[c]
    nchunk = (length + RB - 1) // RB
    g = [g_ref[i:i + 1, :] for i in range(6)]
    lane = lax.broadcasted_iota(jnp.int32, (RES, PAIR), 1)
    hmask = head_mask(PAIR)
    ones_bd = hmask.astype(BF)

    @pl.when(c == 0)
    def _():
        for ref in (d_op, d_tri, d_to, d_pa, d_po, d_p1, d_p2t, d_bb, d_g, d_rel):
            ref[...] = jnp.zeros_like(ref)

    dsides_ref[...] = jnp.zeros_like(dsides_ref)

    @pl.when(nchunk < RES // RB)
    def _():
        dt_scr[...] = jnp.zeros_like(dt_scr)
        a_scr[...] = jnp.zeros_like(a_scr)
        b_scr[...] = jnp.zeros_like(b_scr)

    def gain_add(i, v):
        d_g[i * 8:(i + 1) * 8, :] += jnp.sum(v.reshape(M // 8, 8, PAIR), axis=0)

    def phase_a(ci, _):
        r0 = pl.multiple_of(ci * M, M)
        rows = pl.ds(r0, M)
        x4, r4 = ln_stats(p3_ref[0, rows, :])
        xx = jnp.concatenate([(x4 * g[4]).astype(BF), (x4 * g[5]).astype(BF)], axis=1)
        d_bb[...] += nn(dbt_ref[0, :, rows], xx)
        dxx = nn(db_ref[0, rows, :], w_bb[...])
        da, di = dxx[:, :PAIR], dxx[:, PAIR:]
        gain_add(4, da * x4)
        gain_add(5, di * x4)
        dp = ln_back(da * g[4] + di * g[5], x4, r4)
        dpb = dp.astype(BF)
        d_p2t[...] += tn(dpb, hh_ref[0, rows, 0:512])
        dh = nt(dpb, w_p2[...])
        dhb = (dh * hh_ref[0, rows, 512:1024].astype(F32)).astype(BF)
        x3, r3 = ln_stats(p2_ref[0, rows, :])
        d_p1[...] += tn((x3 * g[3]).astype(BF), dhb)
        dx = nt(dhb, w_p1[...])
        gain_add(3, dx * x3)
        dp = dp + ln_back(dx * g[3], x3, r3)
        dpb = dp.astype(BF)
        sg = pa_ref[0, rows, 384:512].astype(F32)
        o = pa_ref[0, rows, 640:768].astype(F32)
        so = sg * o
        d_po[...] += tn(so.astype(BF), dpb)
        dy = nt(dpb, w_po[...])
        do = dy * sg
        dsg = dy * so * (1.0 - sg)
        dob = do.astype(BF)
        delta = nn((do * o).astype(BF), ones_bd)
        dqkv = []
        for i in range(RB):
            sl = slice(i * RES, (i + 1) * RES)
            ri = pl.ds(pl.multiple_of(r0 + i * RES, RES), RES)
            q = pa_ref[0, ri, 0:128]
            kbd = block_diag(pa_ref[0, ri, 128:256], hmask)
            vbd = block_diag(pa_ref[0, ri, 256:384], hmask)
            p = pa_ref[0, ri, 512:640]
            dpr = nt(dob[sl], vbd)
            ds = (p.astype(F32) * (dpr - delta[sl]) * (32.0 ** -0.5)).astype(BF)
            dq = nn(ds, kbd)
            both = jnp.concatenate([ds, p], axis=1)
            t = tn(both, jnp.concatenate([q, dob[sl]], axis=1))
            dkb = jnp.where(hmask, t[:PAIR, :PAIR], 0.0)
            dvb = jnp.where(hmask, t[PAIR:, PAIR:], 0.0)
            dk = dkb[0:32] + dkb[32:64] + dkb[64:96] + dkb[96:128]
            dv = dvb[0:32] + dvb[32:64] + dvb[64:96] + dvb[96:128]
            dqkv.append(jnp.concatenate([dq.astype(BF), dk.astype(BF), dv.astype(BF)], axis=1))
        dpa = jnp.concatenate([jnp.concatenate(dqkv, axis=0), dsg.astype(BF)], axis=1)
        x2, r2 = ln_stats(p1_ref[0, rows, :])
        d_pa[...] += tn((x2 * g[2]).astype(BF), dpa)
        dx = nt(dpa, w_pa[...])
        gain_add(2, dx * x2)
        dp = dp + ln_back(dx * g[2], x2, r2)
        dp_scr[rows, :] = dp
        xt, rt = ln_stats(tri_ref[0, rows, :])
        xtb = (xt * g[1]).astype(BF)
        u = nn(xtb, w_to[...])
        st = gt_ref[0, rows, 512:640].astype(F32)
        du = dp * st
        dtg_scr[rows, :] = (du * u * (1.0 - st)).astype(BF)
        dub = du.astype(BF)
        d_to[...] += tn(xtb, dub)
        dx = nt(dub, w_to[...])
        gain_add(1, dx * xt)
        dt_scr[rows, :] = ln_back(dx * g[1], xt, rt)
        a_scr[rows, :] = gt_ref[0, rows, 128:256].astype(F32)
        b_scr[rows, :] = gt_ref[0, rows, 384:512].astype(F32)
        return 0

    lax.fori_loop(0, nchunk, phase_a, 0)

    right = sides_ref[0, :, PAIR:]
    IB = 4

    def phase_c(ci, _):
        i0 = pl.multiple_of(ci * RB, RB)
        r0 = pl.multiple_of(ci * M, M)
        rows = pl.ds(r0, M)
        das, dbs = [], []
        for blk in range(RB // IB):
            acc = [jnp.zeros((RES, PAIR), F32) for _ in range(IB)]
            for j in range(RES):
                bj = b_scr[j * RES:(j + 1) * RES, :]
                for u in range(IB):
                    acc[u] = acc[u] + dt_scr[pl.ds((i0 + blk * IB + u) * RES + j, 1), :] * bj
            das += acc
            acc = [jnp.zeros((RES, PAIR), F32) for _ in range(IB)]
            for i in range(RES):
                ai = a_scr[i * RES:(i + 1) * RES, :]
                for u in range(IB):
                    acc[u] = acc[u] + dt_scr[pl.ds(i * RES + i0 + blk * IB + u, 1), :] * ai
            dbs += acc
        da = jnp.concatenate(das, axis=0)
        db = jnp.concatenate(dbs, axis=0)
        jpos = lax.broadcasted_iota(jnp.int32, (RB, RES, PAIR), 1)
        ipos = i0 + lax.broadcasted_iota(jnp.int32, (RB, RES, PAIR), 0)
        pm = ((jpos < length) & (ipos < length)).astype(F32).reshape(M, PAIR)
        sa = gt_ref[0, rows, 0:128].astype(F32)
        sb = gt_ref[0, rows, 256:384].astype(F32)
        a = a_scr[rows, :]
        b = b_scr[rows, :]
        dt = jnp.concatenate([
            (da * a * (1.0 - sa)).astype(BF), (da * sa * pm).astype(BF),
            (db * b * (1.0 - sb)).astype(BF), (db * sb * pm).astype(BF), dtg_scr[rows, :]], axis=1)
        x0, rr = ln_stats(p0_ref[0, rows, :])
        d_tri[...] += tn((x0 * g[0]).astype(BF), dt)
        dx = nt(dt, w_tri[...])
        gain_add(0, dx * x0)
        dp = dp_scr[rows, :] + ln_back(dx * g[0], x0, rr)
        for k in range(RB):
            sl = pl.ds(32 - (i0 + k), RES)
            d_rel[sl, :] += dp[k * RES:(k + 1) * RES]
        dpb = dp.astype(BF)
        left = sides_ref[0, pl.ds(i0, RB), :PAIR]
        outer = (left[:, None, :] * right[None]).reshape(M, PAIR).astype(BF)
        d_op[...] += tn(outer, dpb)
        do = nt(dpb, w_op[...]).reshape(RB, RES, PAIR)
        dsides_ref[0, pl.ds(i0, RB), :PAIR] = jnp.sum(do * right[None], axis=1)
        dsides_ref[0, :, PAIR:] += jnp.sum(do * left[:, None, :], axis=0)
        return 0

    lax.fori_loop(0, nchunk, phase_c, 0)


def pair_backward(lengths, dbt, db, sides, res, w_op, w_tri, w_to, w_pa, w_po, w_p1, w_p2, w_bb, gains):
    crops = sides.shape[0]
    n = RES * RES
    ws = [w_op, w_tri, w_to, w_pa, w_po, w_p1, w_p2, w_bb, gains]
    outs = [(128, 128), (128, 640), (128, 128), (128, 512), (128, 128), (128, 512), (128, 512), (16, 256), (48, 128), (72, 128)]
    ins = [dbt, db, sides, *res]
    return pl.pallas_call(
        bwd_kernel,
        grid_spec=pltpu.PrefetchScalarGridSpec(
            num_scalar_prefetch=1,
            grid=(crops,),
            in_specs=[per_crop(x.shape[1:]) for x in ins] + [full(w.shape) for w in ws],
            out_specs=[per_crop((RES, 256))] + [full(s) for s in outs],
            scratch_shapes=[pltpu.VMEM((n, 128), F32)] * 4 + [pltpu.VMEM((n, 128), BF)],
        ),
        out_shape=[jax.ShapeDtypeStruct((crops, RES, 256), F32)] + [jax.ShapeDtypeStruct(s, F32) for s in outs],
        compiler_params=pltpu.CompilerParams(vmem_limit_bytes=58 << 20),
        name="pair_bwd",
    )(lengths, *ins, *ws)

@jax.custom_vjp
def pair_stack(lengths, sides, pp):
    return pair_run(lengths, sides, pp)[0]


def pair_operands(pp):
    low = {k: v.astype(BF) for k, v in pp.items()}
    zero = jnp.zeros((HEADS, PAIR), BF)
    w_bb = jnp.concatenate(
        [
            jnp.concatenate([low["w_bias"].T, zero], axis=1),
            jnp.concatenate([zero, low["w_ipa_bias"].T], axis=1),
        ],
        axis=0,
    )
    names = ("w_op", "w_tri", "w_tri_out", "w_pa", "w_pa_out", "w_p1", "w_p2")
    return [low[k] for k in names] + [w_bb, pp["g_pair"]]


def pair_run(lengths, sides, pp):
    rel = jnp.pad(pp["w_rel"], ((0, 7), (0, 0)))
    ops = pair_operands(pp)
    both, *res = pair_forward(lengths, sides, rel, *ops)
    return both, (lengths, sides, res, ops)


def pair_back(saved, d_both):
    lengths, sides, res, ops = saved
    d = d_both.astype(BF)
    ds, d_op, d_tri, d_to, d_pa, d_po, d_p1, d_p2t, d_bb, d_g, d_rel = pair_backward(
        lengths, d, jnp.swapaxes(d, 1, 2), sides, res, *ops
    )
    grads = {
        "w_op": d_op,
        "w_tri": d_tri,
        "w_tri_out": d_to,
        "w_pa": d_pa,
        "w_pa_out": d_po,
        "w_p1": d_p1,
        "w_p2": d_p2t.T,
        "w_rel": d_rel[:BINS],
        "w_bias": d_bb[:HEADS, :PAIR].T,
        "w_ipa_bias": d_bb[HEADS:, PAIR:].T,
        "g_pair": d_g.reshape(6, 8, PAIR).sum(1),
    }
    return None, ds, grads


pair_stack.defvjp(pair_run, pair_back)

PAIR_NAMES = ("w_op", "w_tri", "w_tri_out", "w_pa", "w_pa_out", "w_p1", "w_p2", "w_rel", "w_bias", "w_ipa_bias", "g_pair")


def frozen_plm(table, uvz_table, plm_second, tokens, lengths):
    crops, residues = tokens.shape
    one_hot = (tokens[:, :, None] == jnp.arange(VOCAB)[None, None, :]).astype(BF)
    key_mask = (jnp.arange(residues)[None, :] < lengths[:, None])[:, None, :]
    features = product("crv,vp->crp", one_hot, table)
    base = jnp.einsum("crv,vz->crz", one_hot, uvz_table[:, 2 * PLM_FF :].astype(BF))
    gate = jnp.einsum("crv,vz->crz", one_hot.astype(F32), uvz_table[:, :PLM_FF], precision=lax.Precision.HIGHEST)
    value = jnp.einsum("crv,vz->crz", one_hot, uvz_table[:, PLM_FF : 2 * PLM_FF].astype(BF))
    scores = jnp.where(key_mask, product("ciz,cjz->cij", base, base) * PLM_Z ** (-0.5), NEG)
    mixed = product("cij,cje->cie", softmax_last(scores), value)
    plm_out = features + product("cie,ep->cip", gate * mixed, plm_second)
    return layer_norm(plm_out, 1.0).astype(BF)


def crop_loss(params, plm_low, lengths, weight_res, valid, coords):
    multiply = product
    crops, residues = weight_res.shape
    node = multiply("crp,pn->crn", plm_low, params["w_in"])
    gain_node = params["g_node"]
    sides = multiply("crn,nq->crq", layer_norm(node, gain_node[0]), params["w_lr"])
    both = pair_stack(lengths, sides, {k: params[k] for k in PAIR_NAMES})
    both = both.reshape(crops, 2, HEADS, residues, residues)
    bias, ipa_bias = both[:, 0], both[:, 1]
    head_dim = NODE // HEADS
    qkv = (
        multiply("crn,nq->crq", (layer_norm(node, gain_node[1])), params["w_qkv"])
    )
    query = qkv[..., :NODE].reshape(crops, residues, HEADS, head_dim)
    keys = qkv[..., NODE : 2 * NODE].reshape(crops, residues, HEADS, head_dim)
    values = qkv[..., 2 * NODE :].reshape(crops, residues, HEADS, head_dim)
    scores = multiply("cihd,cjhd->chij", query, keys) * head_dim ** (-0.5) + bias
    scores = jnp.where(valid[:, None, None, :] > 0, scores, -1000000000.0)
    attended = multiply("chij,cjhd->cihd", (softmax_last(scores)), values).reshape(
        crops, residues, NODE
    )
    node = node + multiply("crn,nm->crm", (attended), params["w_out"])
    hidden_node = jax.nn.gelu(
        multiply("crn,nf->crf", (layer_norm(node, gain_node[2])), params["w_n1"]),
        approximate=True,
    )
    node = node + multiply("crf,fn->crn", (hidden_node), params["w_n2"])
    start_pos = multiply("crn,nk->crk", (layer_norm(node, gain_node[3])), params["w_s"])
    single = (layer_norm(node, gain_node[4]))
    sqkv = (multiply("crn,nq->crq", single, params["w_ipa"]))
    s_query = sqkv[..., :NODE].reshape(crops, residues, HEADS, head_dim)
    s_keys = sqkv[..., NODE : 2 * NODE].reshape(crops, residues, HEADS, head_dim)
    s_values = sqkv[..., 2 * NODE :].reshape(crops, residues, HEADS, head_dim)
    points = (multiply("crn,nq->crq", single, params["w_pts"])).reshape(
        crops, residues, 2, HEADS, IPA_PTS, 3
    )
    points = points + start_pos[:, :, None, None, None, :]
    point_diff = points[:, :, None, 0] - points[:, None, :, 1]
    dist = jnp.transpose(jnp.sum(point_diff * point_diff, axis=(-1, -2)), (0, 3, 1, 2))
    ipa_scores = (
        multiply("cihd,cjhd->chij", s_query, s_keys) * head_dim ** (-0.5)
        + ipa_bias
        - point_weight * dist
    )
    ipa_scores = jnp.where(valid[:, None, None, :] > 0, ipa_scores, -1000000000.0)
    ipa_att = multiply("chij,cjhd->cihd", (softmax_last(ipa_scores)), s_values).reshape(
        crops, residues, NODE
    )
    node = node + multiply("crn,nm->crm", (ipa_att), params["w_ipa_out"])
    predicted = start_pos + multiply(
        "crn,nk->crk", (layer_norm(node, gain_node[5])), params["w_bb"]
    )
    truth = jnp.transpose(coords, (0, 2, 1))
    pred_diff = predicted[:, :, None, :] - predicted[:, None, :, :]
    true_diff = truth[:, :, None, :] - truth[:, None, :, :]
    dist_pred = jnp.sqrt(jnp.sum(pred_diff * pred_diff, axis=-1) + 1.0)
    dist_true = jnp.sqrt(jnp.sum(true_diff * true_diff, axis=-1) + 1.0)
    error = jnp.sqrt((dist_pred - dist_true) ** 2 + 1.0) - 1.0
    pair_weight = weight_res[:, :, None] * weight_res[:, None, :]
    return jnp.sum(pair_weight * error)


def adam_update(master, first_moment, second_moment, step, grad, norm):
    clipped = grad * jnp.minimum(1.0, clip_norm / norm)
    first = beta_one * first_moment + (1.0 - beta_one) * clipped
    second = beta_two * second_moment + (1.0 - beta_two) * clipped * clipped
    step_count = step[0].astype(jnp.float32)
    first_hat = first / (1.0 - beta_one**step_count)
    second_hat = second / (1.0 - beta_two**step_count)
    updated = master - learn_rate * (
        first_hat / (jnp.sqrt(second_hat) + adam_eps) + decay_rate * master
    )
    return (updated, first, second, updated.astype(jnp.bfloat16))


def local(
    master,
    first_moment,
    second_moment,
    step,
    plm_table,
    plm_first,
    plm_second,
    tokens,
    lengths,
    resolved,
    coords,
):
    table_low = layer_norm(plm_table.astype(F32), 1.0).astype(BF)
    depth = plm_first.shape[0]
    own_table = lax.dynamic_slice_in_dim(table_low, lax.axis_index("shard") * depth, depth, 1)
    uvz_table = jax.nn.silu(lax.psum(product("vp,pe->ve", own_table, plm_first), "shard"))
    frozen_second = lax.all_gather(plm_second, "shard", axis=0, tiled=True)
    gathered = lax.all_gather(master.astype(BF), "shard", axis=0, tiled=True)
    params = unpack(gathered.astype(F32).reshape(-1))
    weight_res, valid = residue_weight(lengths, resolved)
    local_pairs = jnp.sum(jnp.sum(weight_res, axis=1) ** 2)
    plm_low = frozen_plm(plm_table, uvz_table, frozen_second, tokens, lengths)

    def loss_of(weights):
        return crop_loss(weights, plm_low, lengths, weight_res, valid, coords)

    loss_part, pullback = jax.vjp(loss_of, params)
    (grads,) = pullback(jnp.float32(1.0))
    flat = jnp.concatenate([grads[name].reshape(-1) for name, extent in layout()])
    spare = gathered.size - flat.shape[0]
    scalars = jnp.pad(jnp.stack([loss_part, local_pairs]), (0, spare - 2))
    summed = lax.psum(jnp.concatenate([flat, scalars]).reshape(-1, 128), ("crop", "shard"))
    inv_count = 1.0 / summed[-1, 1]
    loss = summed[-1, 0] * inv_count
    live = (jnp.arange(summed.shape[0]) < summed.shape[0] - spare // 128)[:, None]
    summed = jnp.where(live, summed * inv_count, 0.0)
    own_rows = master.shape[0]
    own_grad = lax.dynamic_slice_in_dim(summed, lax.axis_index("shard") * own_rows, own_rows, 0)
    norm = jnp.sqrt(jnp.sum(summed * summed))
    updated, first, second, copy_low = adam_update(
        master, first_moment, second_moment, step, own_grad, norm
    )
    return (updated, first, second, copy_low, loss, norm)


def solution(mesh):
    placed = (
        P("shard", None),
        P("shard", None),
        P("shard", None),
        P(),
        P(),
        P("shard", None),
        P("shard", None),
        P(("crop", "shard"), None),
        P(("crop", "shard")),
        P(("crop", "shard"), None),
        P(("crop", "shard"), None, None),
    )
    return jax.shard_map(
        local,
        mesh=mesh,
        in_specs=placed,
        out_specs=(
            P("shard", None),
            P("shard", None),
            P("shard", None),
            P("shard", None),
            P(),
            P(),
        ),
        check_vma=False,
    )
```

time: 2210 us -> 1210 us (0.55)
  matrix products: 784 us -> 84.1 us
  local copies, waits for them, and re-layouts: 618 us -> 177 us
  other arithmetic: 437 us -> 88.3 us
  Pallas kernels: 0 us -> 317 us
  waiting for transfers between devices: 229 us -> 516 us
  blocking collectives: 84.3 us -> 0 us
  loops' own time: 25.8 us -> 0 us
    dot_general x344 -> x48, matrix products: 780 us -> 78.1 us  [product(): jnp.einsum(form, left.astype(jnp.bfloat16), right.astype(jnp.bfloat16), p...]
    psum x1 -> x2, waiting for transfers between devices: 126 us -> 479 us  [the longest x1 448 us: local(): lax.psum(jnp.concatenate([flat, scalars]).reshape(-1, 128), ('crop', 'sha...]
    pallas_call x0 -> x2, Pallas kernels: none -> 317 us  [the longest x1 168 us: pair_forward(): pl.pallas_call(fwd_kernel, grid_spec=pltpu.PrefetchScalarGridSpec(num_sca...]
    convert_element_type x56 -> x17, local copies, waits for them, and re-layouts: 125 us -> 24.5 us  [product(): right.astype(jnp.bfloat16)]
    reshape x44 -> x16, local copies, waits for them, and re-layouts: 111 us -> 18.9 us  [the longest x12 8.94 us: local(): grads[name].reshape(-1)]
    psum x2 -> x0, blocking collectives: 84.3 us -> none  [the longest x1 42.6 us: local(): total_pairs = lax.psum(local_pairs, ('crop', 'shard'))]
    dot_general x28 -> x2, local copies, waits for them, and re-layouts: 84.9 us -> 0.8 us  [product(): jnp.einsum(form, left.astype(jnp.bfloat16), right.astype(jnp.bfloat16), p...]
    convert_element_type x28 -> x4, local copies, waits for them, and re-layouts: 89.2 us -> 10.2 us  [product(): left.astype(jnp.bfloat16)]
  transfers between devices with their start and end apart: 4 -> 4, of which waited for: 3 -> 4; matrix products, arithmetic and copies ran while one was open for 1% -> 4% of each run, Pallas kernels for 0% -> 0%
where the time goes in v1:
time: 1210 us; the launch traced here: 1200 us
  waiting for transfers between devices  516 us (43%)
  Pallas kernels  317 us (26%)
  local copies, waits for them, and re-layouts  177 us (15%)
  other arithmetic  88.3 us (7%)
  matrix products  84.1 us (7%)
  between operations  20.8 us (2%)
    psum x1, waiting for transfers between devices, local(): lax.psum(jnp.concatenate([flat, scalars]).reshape(-1, 128), ('crop', 'sha...  448 us
    pallas_call x1, Pallas kernels, pair_forward(): pl.pallas_call(fwd_kernel, grid_spec=pltpu.PrefetchScalarGridSpec(num_sca...  168 us
    pallas_call x1, Pallas kernels, crop_loss(): both = pair_stack(lengths, sides, {k: params[k] for k in PAIR_NAMES})  149 us
    dot_general x48, matrix products, product(): jnp.einsum(form, left.astype(jnp.bfloat16), right.astype(jnp.bfloat16), p...  78.1 us
    unnamed x302, local copies, waits for them, and re-layouts  52.3 us
    psum x1, waiting for transfers between devices, local(): lax.psum(product('vp,pe->ve', own_table, plm_first), 'shard')  30.6 us
    convert_element_type x17, local copies, waits for them, and re-layouts, product(): right.astype(jnp.bfloat16)  24.5 us
  transfers between devices with their start and end apart: 4, of which 4 were waited for; matrix products, arithmetic and copies ran while one was open for 4% of the time, Pallas kernels for 0%

profile of v1, /device:TPU:0, one launch (start us, length us, event | category | flops | bytes accessed | tf_op | source)
XLA Modules:
  0.0 1202.6 jit_solution(13295066068763375038)
XLA Ops:
  16.4 30.6 %all-reduce.23.cloned.1.call-done = f32[21,5248]{1,0:T(8,128)} async-done(((f32[21,5248]{1,0:T(8,128)}), f32[21,5248]{1,0:T(8,128)}) %all-reduce.23.cloned.1.call-update) | async-done | bytes 440848 | tf_op jit(solution)/shard_map/psum | solution.py:655
  48.7 3.9 fusion.37
  52.6 5.5 multiply_convert_fusion
  58.1 22.9 %all-gather.6.cloned.1.call-done = bf16[4,3580,128]{2,1,0:T(8,128)(2,1)} async-done(((bf16[1,3580,128]{2,1,0:T(8,128)(2,1)}), bf16[4,3580,128]{2,1,0:T(8,128)(2,1)}) %all-gather.6.cloned.1.call-update) | async-done | bytes 3665936 | tf_op jit(solution)/shard_map/all_gather | solution.py:657
  80.9 3.7 reshape.661
  87.6 6.0 convert_element_type.385
  116.8 13.6 %all-gather.4.cloned.1.call-done = bf16[2560,1280]{1,0:T(8,128)(2,1)} async-done(((bf16[640,1280]{1,0:T(8,128)(2,1)}), bf16[2560,1280]{1,0:T(8,128)(2,1)}) %all-gather.4.cloned.1.call-update) | async-done | bytes 6553616 | tf_op jit(solution)/shard_map/all_gather | solution.py:656
  130.4 6.4 fusion.5
  150.3 167.6 %jvp_pair_fwd_.1 = (f32[16,16,1024]{2,1,0:T(8,128)}, f32[16,1024,128]{2,1,0:T(8,128)}, f32[16,1024,128]{2,1,0:T(8,128)}, f32[16,1024,128]{2,1,0:T(8,128)}, f32[1...) custom-call(s32[16]{0:T(128)} %len_ref.3, ...), custom_call_target="tpu_custom_call" | custom-call | tf_op jit(solution)/shard_map/jvp(pair_fwd)/pallas_call | solution.py:309
  317.8 3.9 reshape.591
  321.8 5.0 fusion.222
  355.8 4.7 copy.197
  360.5 10.4 fusion.1
  374.0 3.8 fusion.239
  390.6 3.7 convolution_convert_fusion.4
  406.4 19.4 %fusion.4 = (f32[16,32,8,4,3]{1,2,4,3,0:T(8,128)}, f32[16,32,8,4,3]{2,4,3,1,0:T(4,128)}) fusion(f32[16,32,32,8]{2,3,1,0:T(8,128)} %copy.208, f32[16,32,8,4,3]{1,2,4,3,0:T(8,128)} %get-tuple-element.122, f32[16,32,8,4,3]{2,4,3,1,0:T(4,128)} %copy.197), kind=kLoop, calls=%fused_computation.6 | loop fusion | flops 7766016 | bytes 1310720 | tf_op jit(solution)/shard_map/transpose(jvp())/reduce_sum | solution.py:601
  427.9 4.5 copy.209
  473.4 3.7 convolution_convert_fusion.2
  487.0 3.9 copy.232
  490.9 3.5 convert_element_type.465.dbt_ref
  497.6 149.4 %transpose_jvp_pair_bwd__.1 = (f32[16,32,256]{2,1,0:T(8,128)}, f32[128,128]{1,0:T(8,128)}, f32[128,640]{1,0:T(8,128)}, f32[128,128]{1,0:T(8,128)}, f32[128,512]{...) custom-call(s32[16]{0:T(128)} %len_ref.3, ...), custom_call_target="tpu_custom_call" | custom-call | tf_op jit(solution)/shard_map/transpose(jvp(pair_bwd))/pallas_call | solution.py:570
  722.4 448.0 %all-reduce.25.cloned.1.call-done = f32[14320,128]{1,0:T(8,128)} async-done(((f32[14320,128]{1,0:T(8,128)}), f32[14320,128]{1,0:T(8,128)}) %all-reduce.25.cloned.1.call-update) | async-done | bytes 7331856 | tf_op jit(solution)/shard_map/psum | solution.py:671
  1173.0 12.7 %multiply_reduce_fusion = (f32[]{:T(128)}, f32[14320,128]{1,0:T(8,128)}) fusion(f32[14320,128]{1,0:T(8,128)} %all-reduce.25.cloned.1.call-done, f32[]{:T(128)} %bitcast.86, pred[14320]{0:T(1024)(128)(4,1)S(1)} %iota_compare_fusion.7), kind=kLoop, calls=%fused_computation.7 | loop fusion | flops 7331839 | bytes 14678008 | tf_op jit(solution)/shard_map/reduce_sum | solution.py:678
  1186.5 7.1 fusion.212
  (499 shorter events, 238.0 us)
Async XLA Ops:
  7.2 39.8 %all-reduce.23.cloned.1.call-start = ((), (), s32[]{:S(2)}) async-start(), calls=%async_computation | async-start | bytes 1007616 | tf_op jit(solution)/shard_map/psum | solution.py:655
  10.9 70.0 %all-gather.6.cloned.1.call-start = ((), (), s32[]{:S(2)}) async-start(), calls=%async_computation.3 | async-start | bytes 4587520 | tf_op jit(solution)/shard_map/all_gather | solution.py:657
  13.5 34.7 %copy-start.93 = (s32[16,32]{1,0:T(8,128)S(1)}, s32[16,32]{1,0:T(8,128)}, u32[]{:S(2)}) copy-start(s32[16,32]{1,0:T(8,128)} %param.18) | copy-start | bytes 6148
  13.5 116.9 %all-gather.4.cloned.1.call-start = ((), (), s32[]{:S(2)}) async-start(), calls=%async_computation.1 | async-start | bytes 8192000 | tf_op jit(solution)/shard_map/all_gather | solution.py:656
  14.3 1156.1 %all-reduce.25.cloned.1.call-start = ((), (), s32[]{:S(2)}) async-start(), calls=%async_computation.2 | async-start | bytes 14663680 | tf_op jit(solution)/shard_map/psum | solution.py:671
  16.4 316.1 %copy-start.90 = (pred[16,32]{1,0:T(8,128)(4,1)}, pred[16,32]{1,0:T(8,128)(4,1)S(1)}, u32[]{:S(2)}) copy-start(pred[16,32]{1,0:T(8,128)(4,1)S(1)} %get-tuple-element.139) | copy-start | bytes 1540
  87.5 9.7 slice-start
  87.6 10.5 slice-start.1
  107.4 23.0 %copy-start.29 = (bf16[16,32,2560]{2,1,0:T(8,128)(2,1)S(1)}, bf16[16,32,2560]{2,1,0:T(8,128)(2,1)}, u32[]{:S(2)}) copy-start(bf16[16,32,2560]{2,1,0:T(8,128)(2,1)} %multiply_convert_fusion) | copy-start | bytes 7864324
  115.4 24.2 %copy-start.122 = (f32[256]{0:T(256)}, f32[256]{0:T(256)S(1)}, u32[]{:S(2)}) copy-start(f32[256]{0:T(256)S(1)} %get-tuple-element.97) | copy-start | bytes 3076
  115.4 32.8 %copy-start.124 = (f32[256]{0:T(256)}, f32[256]{0:T(256)S(1)}, u32[]{:S(2)}) copy-start(f32[256]{0:T(256)S(1)} %get-tuple-element.96) | copy-start | bytes 3076
  116.8 20.0 %copy-start.66 = (bf16[21,1280]{1,0:T(8,128)(2,1)S(1)}, bf16[21,1280]{1,0:T(8,128)(2,1)}, u32[]{:S(2)}) copy-start(bf16[21,1280]{1,0:T(8,128)(2,1)} %param.15) | copy-start | bytes 161284
  139.2 199.1 %copy-start.7 = (f32[16,32,256]{2,1,0:T(8,128)}, f32[16,32,256]{2,1,0:T(8,128)S(1)}, u32[]{:S(2)}) copy-start(f32[16,32,256]{2,1,0:T(8,128)S(1)} %get-tuple-element.146) | copy-start | bytes 1572868
  139.2 9.0 copy-start.84
  139.5 8.7 copy-start.86
  434.9 7.7 copy-start.74
  497.6 149.4 %copy-start.8 = (f32[16,32,256]{2,1,0:T(8,128)S(1)}, f32[16,32,256]{2,1,0:T(8,128)}, u32[]{:S(2)}) copy-start(f32[16,32,256]{2,1,0:T(8,128)} %copy-done.7) | copy-start | bytes 1572868
  497.6 149.4 %copy-start.85 = (f32[16,32]{1,0:T(8,128)S(1)}, f32[16,32]{1,0:T(8,128)}, u32[]{:S(2)}) copy-start(f32[16,32]{1,0:T(8,128)} %copy-done.84) | copy-start | bytes 6148
  497.6 149.4 %copy-start.87 = (f32[16,32]{1,0:T(8,128)S(1)}, f32[16,32]{1,0:T(8,128)}, u32[]{:S(2)}) copy-start(f32[16,32]{1,0:T(8,128)} %copy-done.86) | copy-start | bytes 6148
  497.6 149.4 %copy-start.125 = (f32[256]{0:T(256)S(1)}, f32[256]{0:T(256)}, u32[]{:S(2)}) copy-start(f32[256]{0:T(256)} %copy-done.124) | copy-start | bytes 3076
  667.9 8.1 copy-start.123
  699.2 9.2 copy-start.27
  702.2 11.2 copy-start.50
  702.8 12.2 %copy-start.121 = (f32[768]{0:T(1024)S(1)}, f32[768]{0:T(1024)}, u32[]{:S(2)}) copy-start(f32[768]{0:T(1024)} %reshape.659) | copy-start | bytes 9220
  (116 other events, 319.8 us)
Sparse Core Ops, SparseCore 0:
  11.0 35.9 all-reduce.22
  49.1 31.7 all-gather.5
  82.5 47.8 all-gather.3
  721.7 448.5 all-reduce.24
